TPU v7x, 256 devices: a whole 4x4x8 slice. The times are simulated.
256 devices in a mesh: sens: 4 (over y), samp: 64 (over z, x, core).
Axes of the slice: x: 4, y: 4, z: 8, core: 2. Of those that a mesh axis runs over, the one named last changes fastest.
Arguments:
- slopes: bfloat16 [2, 256, 150528], P(None, 'samp', 'sens'), may hold values from -0.0625 to 0.0625
- targets: bfloat16 [2, 16384, 256], P(None, 'samp'), may hold values from -6 to 6
- reconstructor: float32 [4, 64, 32, 128, 128], P('sens', 'samp'), may hold values from -6 to 6
- foot_act: int32 [4, 64, 32], P('sens'), may hold values from 0 to 1, as said below
- foot_slope: int32 [4, 64, 32], P('sens'), may hold values from 0 to 293, as said below
- foot_count: int32 [4, 64], P('sens'), may hold values from 16 to 32, as said below
Outputs:
- fitted: float32 [4, 64, 32, 128, 128], P('sens', 'samp')
- fit_residual: bfloat16 [16384, 256], P('samp')
Inputs may be any that keep to these rules, and one draw needn't show every extreme that they name: `foot_act`: slots 0 to foot_count-1 of a device are live, the rest padding (actuator block 0 and a slope block already named by slot 0); no (actuator block, slope block) pair repeats among live slots; the slope blocks of one actuator block form a run of consecutive blocks modulo 294. `foot_slope`: the live slots of one device name at most 20 distinct slope blocks; for every sens index some device names exactly 20. `foot_count`: for every sens index some device has 32 live slots.
All inputs are finite; a program needn't handle non-finite values.
Results may differ from a plain program's by a relative error of at most 0.0037.
Values may be sent and summed in bfloat16 or wider, within the bound.
A program may use at most 64 MiB of HBM per device.

v0:
```python
import jax
import jax.numpy as jnp
from jax import lax
from jax.sharding import PartitionSpec as P

STEPS = 2


def per_device(slopes, targets, reconstructor, foot_act, foot_slope, foot_count):
    samp_count = lax.axis_size("samp")
    own_index = lax.axis_index("samp")
    block_size = reconstructor.shape[-1]
    slot_count = reconstructor.shape[2]
    groups = slopes.shape[2] // block_size
    samp_dev = slopes.shape[1]
    act_blocks = targets.shape[1] // block_size
    samples = targets.shape[2]
    step_rate = slot_count * block_size / (samples + 3 * slot_count * block_size)
    act_all = foot_act[0]
    slope_all = foot_slope[0]
    count_all = foot_count[0]
    live_all = jnp.arange(slot_count)[None, :] < count_all[:, None]
    own_act = lax.dynamic_index_in_dim(act_all, own_index, 0, keepdims=False)
    own_live = lax.dynamic_index_in_dim(live_all, own_index, 0, keepdims=False)
    act_onehot = ((own_act[None, :] == jnp.arange(act_blocks)[:, None]) & own_live[None, :]).astype(
        jnp.float32
    )
    need_count = slope_all.shape[1]
    weights = reconstructor[0, 0]
    fit_residual = None
    for step in range(STEPS):
        local_rows = slopes[step].reshape(samp_dev, groups, block_size)
        outgoing = jnp.take(local_rows, slope_all.reshape(-1), axis=1)
        outgoing = outgoing.reshape(samp_dev, samp_count, need_count, block_size)
        arrived = lax.all_to_all(outgoing, "samp", split_axis=1, concat_axis=0, tiled=True)
        slot_slopes = arrived.reshape(samples, need_count, block_size)
        weights_low = weights.astype(jnp.bfloat16)
        partial_sums = jnp.einsum(
            "kil,nkl->kin", weights_low, slot_slopes, preferred_element_type=jnp.float32
        )
        summed = jnp.einsum(
            "jk,kin->jin", act_onehot, partial_sums, precision=lax.Precision.HIGHEST
        )
        target_now = targets[step].reshape(act_blocks, block_size, samples)
        total = lax.psum(summed, "sens")
        residual = (total - target_now).astype(jnp.bfloat16)
        slot_residual = jnp.take(residual, own_act, axis=0)
        gradient = jnp.einsum(
            "kin,nkl->kil", slot_residual, slot_slopes, preferred_element_type=jnp.float32
        )
        weights = jnp.where(own_live[:, None, None], weights - step_rate * gradient, weights)
        fit_residual = residual
    return (weights[None, None], fit_residual.reshape(act_blocks * block_size, samples))


def solution(mesh):
    return jax.shard_map(
        per_device,
        mesh=mesh,
        in_specs=(
            P(None, "samp", "sens"),
            P(None, "samp", None),
            P("sens", "samp", None, None, None),
            P("sens", None, None),
            P("sens", None, None),
            P("sens", None),
        ),
        out_specs=(P("sens", "samp", None, None, None), P("samp", None)),
        check_vma=False,
    )
```

profile of v0, /device:TPU:2, one launch (start us, length us, event | category | flops | bytes accessed | tf_op | source)
XLA Modules:
  0.0 260.0 jit_solution(15203739831678689904)
XLA Ops:
  7.2 0.8 copy.50
  8.1 1.3 slice_bitcast_fusion
  9.4 14.6 %gather_fusion.2 = bf16[2048,4,128]{2,1,0:T(4,128)(2,1)} fusion(bf16[4,294,128]{2,0,1:T(4,128)(2,1)S(1)} %get-tuple-element.4, s32[2048]{0:T(1024)S(1)} %fusion.19), kind=kCustom, calls=%fused_computation.2.clone | custom fusion | bytes 4202496 | tf_op jit(solution)/shard_map/jit(_take)/gather | solution.py:33
  24.0 14.5 %gather_fusion = bf16[2048,4,128]{2,1,0:T(4,128)(2,1)} fusion(bf16[4,294,128]{2,0,1:T(4,128)(2,1)S(1)} %get-tuple-element.5, s32[2048]{0:T(1024)S(1)} %fusion.19), kind=kCustom, calls=%fused_computation.clone | custom fusion | bytes 4202496 | tf_op jit(solution)/shard_map/jit(_take)/gather | solution.py:33
  38.4 10.6 %broadcast_select_fusion = (bf16[2048,4,128]{2,1,0:T(4,128)(2,1)S(1)}, bf16[2048,4,128]{2,1,0:T(4,128)(2,1)S(1)}) fusion(bf16[2048,4,128]{2,1,0:T(4,128)(2,1)} %gather_fusion.2, pred[2048]{0:T(1024)(128)(4,1)S(1)} %compare_and_fusion, bf16[2048,4,128]{2,1,0:T(4,128)(2,1)} %gather_fusion), kind=kLoop, calls=%fused_computation.15 | loop fusion | flops 2097152 | bytes 8390656 | tf_op jit(solution)/shard_map/jit(_take)/select_n | solution.py:33
  49.0 1.9 copy.53
  50.9 12.2 %all-to-all-start = ((bf16[4,64,32,128]{3,2,0,1:T(8,128)(2,1)}), bf16[4,64,32,128]{3,2,0,1:T(8,128)(2,1)}, u32[]{:S(2)}, u32[]{:S(2)}) async-start(bf16[4,64,32,128]{3,2,0,1:T(8,128)(2,1)} %copy.53), calls=%async_computation | async-start | bytes 4194304 | tf_op jit(solution)/shard_map/all_to_all | solution.py:35
  63.1 1.9 copy.59
  65.1 49.2 %all-to-all-done = bf16[4,64,32,128]{3,2,0,1:T(8,128)(2,1)} async-done(((bf16[4,64,32,128]{3,2,0,1:T(8,128)(2,1)}), bf16[4,64,32,128]{3,2,0,1:T(8,128)(2,1)}, u32[]{:S(2)}, u32[]{:S(2)}) %all-to-all-start) | async-done | bytes 2097184 | tf_op jit(solution)/shard_map/all_to_all | solution.py:35
  114.3 5.4 %all-to-all-start.1 = ((bf16[4,64,32,128]{3,2,0,1:T(8,128)(2,1)}), bf16[4,64,32,128]{3,2,0,1:T(8,128)(2,1)S(1)}, u32[]{:S(2)}, u32[]{:S(2)}) async-start(bf16[4,64,32,128]{3,2,0,1:T(8,128)(2,1)} %copy.59), calls=%async_computation.1 | async-start | bytes 4194304 | tf_op jit(solution)/shard_map/all_to_all | solution.py:35
  119.8 0.6 dynamic-slice.1
  120.6 0.7 compare_bitcast_fusion
  121.3 2.8 %copy.54 = bf16[64,4,1,32,128]{4,1,0,3,2:T(4,128)(2,1)S(1)} copy(bf16[64,4,1,32,128]{4,3,1,0,2:T(8,128)(2,1)} %bitcast.8) | data formatting | bytes 4194304 | tf_op jit(solution)/shard_map/all_to_all | solution.py:35
  124.1 1.3 copy-done.2
  125.4 2.7 %convolution_bitcast_fusion = f32[32,128,256]{1,2,0:T(8,128)} fusion(bf16[256,32,128]{2,0,1:T(8,128)(2,1)S(1)} %bitcast.54, f32[1,1,32,128,128]{4,3,2,1,0:T(8,128)S(1)} %copy-done.4), kind=kOutput, calls=%fused_computation.8 | convolution fusion | flops 268435456 | bytes 8388608 | tf_op jit(solution)/shard_map/kil,nkl->kin/dot_general | solution.py:38
  128.1 5.5 %copy.55 = f32[32,128,256]{2,0,1:T(8,128)} copy(f32[32,128,256]{1,2,0:T(8,128)} %convolution_bitcast_fusion) | data formatting | bytes 8388608 | tf_op jit(solution)/shard_map/kil,nkl->kin/dot_general | solution.py:38
  133.6 3.7 %fusion.21 = f32[2,128,256]{2,0,1:T(2,128)S(1)} fusion(f32[32,128,256]{2,0,1:T(8,128)} %copy.55, pred[32]{0:T(512)(128)(4,1)S(1)} %compare_bitcast_fusion, s32[32]{0:T(128)S(1)} %dynamic-slice_reduce_fusion), kind=kOutput, calls=%fused_computation.36 | convolution fusion | flops 25165952 | bytes 4456608 | tf_op jit(solution)/shard_map/jk,kin->jin/dot_general | solution.py:41
  137.3 0.7 copy.56
  138.0 0.2 all-reduce.5.cloned.1.call-start
  138.3 32.7 %all-to-all-done.1 = bf16[4,64,32,128]{3,2,0,1:T(8,128)(2,1)S(1)} async-done(((bf16[4,64,32,128]{3,2,0,1:T(8,128)(2,1)}), bf16[4,64,32,128]{3,2,0,1:T(8,128)(2,1)S(1)}, u32[]{:S(2)}, u32[]{:S(2)}) %all-to-all-start.1) | async-done | bytes 2097184 | tf_op jit(solution)/shard_map/all_to_all | solution.py:35
  171.0 2.4 copy.60
  173.4 12.8 %all-reduce.3.cloned.1.call-done = f32[2,128,256]{2,1,0:T(8,128)} async-done(((f32[2,128,256]{2,1,0:T(8,128)}), f32[2,128,256]{2,1,0:T(8,128)}) %all-reduce.3.cloned.1.call-update) | async-done | bytes 262160 | tf_op jit(solution)/shard_map/psum | solution.py:45
  186.2 1.0 fusion.18
  187.2 2.0 gather_fusion.1
  189.2 3.8 %subtract_select_fusion.1 = f32[32,128,128]{2,1,0:T(8,128)S(1)} fusion(f32[1,1,32,128,128]{4,3,2,1,0:T(8,128)} %param.12, bf16[256,32,128]{2,0,1:T(8,128)(2,1)} %bitcast.55, bf16[32,128,256]{2,1,0:T(8,128)(2,1)} %gather_fusion.1, pred[32]{0:T(512)(128)(4,1)S(1)} %compare_and_fusion.1, pred[32]{0:T(512)(128)(4,1)S(1)} %compare_bitcast_fusion), kind=kOutput, calls=%fused_computation.7 | convolution fusion | flops 271056896 | bytes 8388672 | tf_op jit(solution)/shard_map/kin,nkl->kil/dot_general | solution.py:48
  193.0 0.7 fusion.15
  193.8 3.8 %fusion = f32[2,128,256]{2,0,1:T(2,128)S(1)} fusion(f32[32,128,256]{2,1,0:T(8,128)S(1)} %fusion.15, pred[32]{0:T(512)(128)(4,1)S(1)} %compare_bitcast_fusion, s32[32]{0:T(128)S(1)} %dynamic-slice_reduce_fusion), kind=kOutput, calls=%fused_computation.4 | convolution fusion | flops 25165952 | bytes 4456608 | tf_op jit(solution)/shard_map/jk,kin->jin/dot_general | solution.py:41
  197.6 0.7 copy.62
  198.3 47.4 %all-reduce.5.cloned.1.call-done = f32[2,128,256]{2,1,0:T(8,128)} async-done(((f32[2,128,256]{2,1,0:T(8,128)}), f32[2,128,256]{2,1,0:T(8,128)}) %all-reduce.5.cloned.1.call-update) | async-done | bytes 262160 | tf_op jit(solution)/shard_map/psum | solution.py:45
  245.8 1.0 fusion.17
  246.7 2.0 gather_fusion.3
  248.8 4.4 %fusion.2 = f32[1,1,32,128,128]{4,3,2,1,0:T(8,128)} fusion(f32[32,128,128]{2,1,0:T(8,128)S(1)} %subtract_select_fusion.1, bf16[256,32,128]{2,0,1:T(8,128)(2,1)} %bitcast.56, bf16[32,128,256]{2,1,0:T(8,128)(2,1)} %gather_fusion.3, pred[32]{0:T(512)(128)(4,1)S(1)} %compare_and_fusion.1, pred[32]{0:T(512)(128)(4,1)S(1)} %compare_bitcast_fusion), kind=kOutput, calls=%fused_computation.9 | convolution fusion | flops 271056896 | bytes 8388672 | tf_op jit(solution)/shard_map/kin,nkl->kil/dot_general | solution.py:48
  (24 shorter events, 0.4 us)
Async XLA Ops:
  7.2 113.3 %copy-start = (s32[1,64,32]{1,2,0:T(8,128)S(1)}, s32[1,64,32]{1,2,0:T(8,128)}, u32[]{:S(2)}) copy-start(s32[1,64,32]{1,2,0:T(8,128)} %param.13) | copy-start | bytes 24580
  50.9 63.4 %all-to-all-start = ((bf16[4,64,32,128]{3,2,0,1:T(8,128)(2,1)}), bf16[4,64,32,128]{3,2,0,1:T(8,128)(2,1)}, u32[]{:S(2)}, u32[]{:S(2)}) async-start(bf16[4,64,32,128]{3,2,0,1:T(8,128)(2,1)} %copy.53), calls=%async_computation | async-start | bytes 4194304 | tf_op jit(solution)/shard_map/all_to_all | solution.py:35
  65.1 54.7 %copy-start.6 = (s32[1,64]{1,0:T(1,128)S(1)}, s32[1,64]{1,0:T(1,128)}, u32[]{:S(2)}) copy-start(s32[1,64]{1,0:T(1,128)} %param.15) | copy-start | bytes 772
  114.3 56.7 %all-to-all-start.1 = ((bf16[4,64,32,128]{3,2,0,1:T(8,128)(2,1)}), bf16[4,64,32,128]{3,2,0,1:T(8,128)(2,1)S(1)}, u32[]{:S(2)}, u32[]{:S(2)}) async-start(bf16[4,64,32,128]{3,2,0,1:T(8,128)(2,1)} %copy.59), calls=%async_computation.1 | async-start | bytes 4194304 | tf_op jit(solution)/shard_map/all_to_all | solution.py:35
  119.8 66.4 %all-reduce.3.cloned.1.call-start = ((), (), s32[]{:S(2)}) async-start(), calls=%async_computation.2 | async-start | bytes 524288 | tf_op jit(solution)/shard_map/psum | solution.py:45
  121.3 4.2 %copy-start.4 = (f32[1,1,32,128,128]{4,3,2,1,0:T(8,128)S(1)}, f32[1,1,32,128,128]{4,3,2,1,0:T(8,128)}, u32[]{:S(2)}) copy-start(f32[1,1,32,128,128]{4,3,2,1,0:T(8,128)} %param.12) | copy-start | bytes 6291460
  124.1 1.3 copy-start.2
  133.6 4.7 %copy-start.5 = (bf16[2,256,256]{2,1,0:T(8,128)(2,1)S(1)}, bf16[2,256,256]{2,1,0:T(8,128)(2,1)}, u32[]{:S(2)}) copy-start(bf16[2,256,256]{2,1,0:T(8,128)(2,1)} %param.11) | copy-start | bytes 786436
  138.0 107.7 %all-reduce.5.cloned.1.call-start = ((), (), s32[]{:S(2)}) async-start(), calls=%async_computation.3 | async-start | bytes 524288 | tf_op jit(solution)/shard_map/psum | solution.py:45
  189.2 3.9 %copy-start.3 = (bf16[64,4,1,32,128]{4,1,0,3,2:T(4,128)(2,1)S(1)}, bf16[64,4,1,32,128]{4,1,0,3,2:T(4,128)(2,1)}, u32[]{:S(2)}) copy-start(bf16[64,4,1,32,128]{4,1,0,3,2:T(4,128)(2,1)} %copy.60) | copy-start | bytes 6291460
  246.7 2.0 copy-start.1
Sparse Core Ops, SparseCore 0:
  138.1 48.0 all-reduce.2
  198.5 47.2 all-reduce.4
where the time goes:
time: 261 us; the launch traced here: 260 us
  waiting for transfers between devices  142 us (54%)
  local copies, waits for them, and re-layouts  53.4 us (20%)
  matrix products  19.1 us (7%)
  starting transfers between devices  17.9 us (7%)
  between operations  14.2 us (5%)
  other arithmetic  13.2 us (5%)
    all_to_all x2, waiting for transfers between devices, per_device(): lax.all_to_all(outgoing, 'samp', split_axis=1, concat_axis=0, tiled=True)  82 us
    psum x2, waiting for transfers between devices, per_device(): total = lax.psum(summed, 'sens')  60.2 us
    gather x2, local copies, waits for them, and re-layouts, per_device(): outgoing = jnp.take(local_rows, slope_all.reshape(-1), axis=1)  29.1 us
    all_to_all x2, starting transfers between devices, per_device(): lax.all_to_all(outgoing, 'samp', split_axis=1, concat_axis=0, tiled=True)  17.6 us
    select_n x1, other arithmetic, per_device(): outgoing = jnp.take(local_rows, slope_all.reshape(-1), axis=1)  10.6 us
    dot_general x2, matrix products, per_device(): jnp.einsum('kin,nkl->kil', slot_residual, slot_slopes, preferred_element_...  8.22 us
    dot_general x2, matrix products, per_device(): jnp.einsum('jk,kin->jin', act_onehot, partial_sums, precision=lax.Precisi...  7.5 us
    dot_general x1, local copies, waits for them, and re-layouts, per_device(): jnp.einsum('kil,nkl->kin', weights_low, slot_slopes, preferred_element_ty...  5.48 us
  transfers between devices with their start and end apart: 4, of which 4 were waited for; matrix products, arithmetic and copies ran while one was open for 8% of the time, Pallas kernels for 0%

commit v1 on v0

--- a/solution.py
+++ b/solution.py
@@ -42,7 +42,7 @@
             "jk,kin->jin", act_onehot, partial_sums, precision=lax.Precision.HIGHEST
         )
         target_now = targets[step].reshape(act_blocks, block_size, samples)
-        total = lax.psum(summed, "sens")
+        total = jnp.sum(lax.all_gather(summed, "sens"), axis=0)
         residual = (total - target_now).astype(jnp.bfloat16)
         slot_residual = jnp.take(residual, own_act, axis=0)
         gradient = jnp.einsum(

time: 261 us -> 225 us (0.86)
  waiting for transfers between devices: 142 us -> 105 us
    psum x2 -> x0, waiting for transfers between devices: 60.2 us -> none  [per_device(): total = lax.psum(summed, 'sens')]
    all_gather x0 -> x2, waiting for transfers between devices: none -> 23.1 us  [per_device(): total = jnp.sum(lax.all_gather(summed, 'sens'), axis=0)]
    reduce_sum x0 -> x2, other arithmetic: none -> 2.64 us  [per_device(): total = jnp.sum(lax.all_gather(summed, 'sens'), axis=0)]
  transfers between devices with their start and end apart: 4 -> 4, of which waited for: 4 -> 3; matrix products, arithmetic and copies ran while one was open for 8% -> 9% of each run, Pallas kernels for 0% -> 0%
where the time goes in v1:
time: 225 us; the launch traced here: 224 us
  waiting for transfers between devices  105 us (47%)
  local copies, waits for them, and re-layouts  53.4 us (24%)
  matrix products  19.1 us (8%)
  starting transfers between devices  17.9 us (8%)
  other arithmetic  14.7 us (7%)
  between operations  14.2 us (6%)
    all_to_all x2, waiting for transfers between devices, per_device(): lax.all_to_all(outgoing, 'samp', split_axis=1, concat_axis=0, tiled=True)  82 us
    gather x2, local copies, waits for them, and re-layouts, per_device(): outgoing = jnp.take(local_rows, slope_all.reshape(-1), axis=1)  29.2 us
    all_gather x2, waiting for transfers between devices, per_device(): total = jnp.sum(lax.all_gather(summed, 'sens'), axis=0)  23.1 us
    all_to_all x2, starting transfers between devices, per_device(): lax.all_to_all(outgoing, 'samp', split_axis=1, concat_axis=0, tiled=True)  17.6 us
    select_n x1, other arithmetic, per_device(): outgoing = jnp.take(local_rows, slope_all.reshape(-1), axis=1)  10.6 us
    dot_general x2, matrix products, per_device(): jnp.einsum('kin,nkl->kil', slot_residual, slot_slopes, preferred_element_...  8.22 us
    dot_general x2, matrix products, per_device(): jnp.einsum('jk,kin->jin', act_onehot, partial_sums, precision=lax.Precisi...  7.5 us
    dot_general x1, local copies, waits for them, and re-layouts, per_device(): jnp.einsum('kil,nkl->kin', weights_low, slot_slopes, preferred_element_ty...  5.48 us
  transfers between devices with their start and end apart: 4, of which 3 were waited for; matrix products, arithmetic and copies ran while one was open for 9% of the time, Pallas kernels for 0%

profile of v1, /device:TPU:2, one launch (start us, length us, event | category | flops | bytes accessed | tf_op | source)
XLA Modules:
  0.0 224.4 jit_solution(10309722219496960412)
XLA Ops:
  7.2 0.8 copy.32
  8.1 1.3 slice_bitcast_fusion
  9.4 14.6 %gather_fusion.2 = bf16[2048,4,128]{2,1,0:T(4,128)(2,1)} fusion(bf16[4,294,128]{2,0,1:T(4,128)(2,1)S(1)} %get-tuple-element.4, s32[2048]{0:T(1024)S(1)} %fusion.19), kind=kCustom, calls=%fused_computation.2.clone | custom fusion | bytes 4202496 | tf_op jit(solution)/shard_map/jit(_take)/gather | solution.py:33
  24.0 14.6 %gather_fusion = bf16[2048,4,128]{2,1,0:T(4,128)(2,1)} fusion(bf16[4,294,128]{2,0,1:T(4,128)(2,1)S(1)} %get-tuple-element.5, s32[2048]{0:T(1024)S(1)} %fusion.19), kind=kCustom, calls=%fused_computation.clone | custom fusion | bytes 4202496 | tf_op jit(solution)/shard_map/jit(_take)/gather | solution.py:33
  38.5 10.6 %broadcast_select_fusion = (bf16[2048,4,128]{2,1,0:T(4,128)(2,1)S(1)}, bf16[2048,4,128]{2,1,0:T(4,128)(2,1)S(1)}) fusion(bf16[2048,4,128]{2,1,0:T(4,128)(2,1)} %gather_fusion.2, pred[2048]{0:T(1024)(128)(4,1)S(1)} %compare_and_fusion, bf16[2048,4,128]{2,1,0:T(4,128)(2,1)} %gather_fusion), kind=kLoop, calls=%fused_computation.15 | loop fusion | flops 2097152 | bytes 8390656 | tf_op jit(solution)/shard_map/jit(_take)/select_n | solution.py:33
  49.1 1.9 copy.35
  51.0 12.2 %all-to-all-start = ((bf16[4,64,32,128]{3,2,0,1:T(8,128)(2,1)}), bf16[4,64,32,128]{3,2,0,1:T(8,128)(2,1)}, u32[]{:S(2)}, u32[]{:S(2)}) async-start(bf16[4,64,32,128]{3,2,0,1:T(8,128)(2,1)} %copy.35), calls=%async_computation | async-start | bytes 4194304 | tf_op jit(solution)/shard_map/all_to_all | solution.py:35
  63.2 1.9 copy.43
  65.2 49.2 %all-to-all-done = bf16[4,64,32,128]{3,2,0,1:T(8,128)(2,1)} async-done(((bf16[4,64,32,128]{3,2,0,1:T(8,128)(2,1)}), bf16[4,64,32,128]{3,2,0,1:T(8,128)(2,1)}, u32[]{:S(2)}, u32[]{:S(2)}) %all-to-all-start) | async-done | bytes 2097184 | tf_op jit(solution)/shard_map/all_to_all | solution.py:35
  114.4 5.4 %all-to-all-start.1 = ((bf16[4,64,32,128]{3,2,0,1:T(8,128)(2,1)}), bf16[4,64,32,128]{3,2,0,1:T(8,128)(2,1)S(1)}, u32[]{:S(2)}, u32[]{:S(2)}) async-start(bf16[4,64,32,128]{3,2,0,1:T(8,128)(2,1)} %copy.43), calls=%async_computation.1 | async-start | bytes 4194304 | tf_op jit(solution)/shard_map/all_to_all | solution.py:35
  119.9 0.6 dynamic-slice.1
  120.7 0.7 compare_bitcast_fusion
  121.4 2.8 %copy.36 = bf16[64,4,1,32,128]{4,1,0,3,2:T(4,128)(2,1)S(1)} copy(bf16[64,4,1,32,128]{4,3,1,0,2:T(8,128)(2,1)} %bitcast.8) | data formatting | bytes 4194304 | tf_op jit(solution)/shard_map/all_to_all | solution.py:35
  124.2 1.3 copy-done.2
  125.5 2.7 %convolution_bitcast_fusion = f32[32,128,256]{1,2,0:T(8,128)} fusion(bf16[256,32,128]{2,0,1:T(8,128)(2,1)S(1)} %bitcast.61, f32[1,1,32,128,128]{4,3,2,1,0:T(8,128)S(1)} %copy-done.3), kind=kOutput, calls=%fused_computation.8 | convolution fusion | flops 268435456 | bytes 8388608 | tf_op jit(solution)/shard_map/kil,nkl->kin/dot_general | solution.py:38
  128.2 5.5 %copy.37 = f32[32,128,256]{2,0,1:T(8,128)} copy(f32[32,128,256]{1,2,0:T(8,128)} %convolution_bitcast_fusion) | data formatting | bytes 8388608 | tf_op jit(solution)/shard_map/kil,nkl->kin/dot_general | solution.py:38
  133.6 3.7 %fusion.21 = f32[2,128,256]{2,0,1:T(2,128)S(1)} fusion(f32[32,128,256]{2,0,1:T(8,128)} %copy.37, pred[32]{0:T(512)(128)(4,1)S(1)} %compare_bitcast_fusion, s32[32]{0:T(128)S(1)} %dynamic-slice_reduce_fusion), kind=kOutput, calls=%fused_computation.38 | convolution fusion | flops 25165952 | bytes 4456608 | tf_op jit(solution)/shard_map/jk,kin->jin/dot_general | solution.py:41
  137.3 0.7 copy.38
  138.1 0.2 all-gather.7.cloned.1.call-start
  138.4 32.7 %all-to-all-done.1 = bf16[4,64,32,128]{3,2,0,1:T(8,128)(2,1)S(1)} async-done(((bf16[4,64,32,128]{3,2,0,1:T(8,128)(2,1)}), bf16[4,64,32,128]{3,2,0,1:T(8,128)(2,1)S(1)}, u32[]{:S(2)}, u32[]{:S(2)}) %all-to-all-start.1) | async-done | bytes 2097184 | tf_op jit(solution)/shard_map/all_to_all | solution.py:35
  171.1 2.4 %copy.44 = bf16[64,4,1,32,128]{4,1,0,3,2:T(4,128)(2,1)} copy(bf16[64,4,1,32,128]{4,3,1,0,2:T(8,128)(2,1)S(1)} %bitcast.65) | data formatting | bytes 4194304 | tf_op jit(solution)/shard_map/all_to_all | solution.py:35
  173.5 1.3 reduce_sum.20
  174.9 2.0 gather_fusion.1
  176.9 3.8 %subtract_select_fusion.1 = f32[32,128,128]{2,1,0:T(8,128)S(1)} fusion(f32[1,1,32,128,128]{4,3,2,1,0:T(8,128)} %param.12, bf16[256,32,128]{2,0,1:T(8,128)(2,1)} %bitcast.62, bf16[32,128,256]{2,1,0:T(8,128)(2,1)} %gather_fusion.1, pred[32]{0:T(512)(128)(4,1)S(1)} %compare_and_fusion.1, pred[32]{0:T(512)(128)(4,1)S(1)} %compare_bitcast_fusion), kind=kOutput, calls=%fused_computation.7 | convolution fusion | flops 271056896 | bytes 8388672 | tf_op jit(solution)/shard_map/kin,nkl->kil/dot_general | solution.py:48
  180.7 0.7 fusion.15
  181.5 3.8 %fusion = f32[2,128,256]{2,0,1:T(2,128)S(1)} fusion(f32[32,128,256]{2,1,0:T(8,128)S(1)} %fusion.15, pred[32]{0:T(512)(128)(4,1)S(1)} %compare_bitcast_fusion, s32[32]{0:T(128)S(1)} %dynamic-slice_reduce_fusion), kind=kOutput, calls=%fused_computation.4 | convolution fusion | flops 25165952 | bytes 4456608 | tf_op jit(solution)/shard_map/jk,kin->jin/dot_general | solution.py:41
  185.3 0.7 copy.46
  186.0 23.1 %all-gather.7.cloned.1.call-done = f32[8,128,256]{2,1,0:T(8,128)} async-done(((f32[2,128,256]{2,1,0:T(8,128)}), f32[8,128,256]{2,1,0:T(8,128)}) %all-gather.7.cloned.1.call-update) | async-done | bytes 1048592 | tf_op jit(solution)/shard_map/all_gather | solution.py:45
  209.1 1.3 reduce_sum.21
  210.4 0.7 fusion.18
  211.1 2.0 gather_fusion.3
  213.2 4.4 %fusion.2 = f32[1,1,32,128,128]{4,3,2,1,0:T(8,128)} fusion(f32[32,128,128]{2,1,0:T(8,128)S(1)} %subtract_select_fusion.1, bf16[256,32,128]{2,0,1:T(8,128)(2,1)} %bitcast.59, bf16[32,128,256]{2,1,0:T(8,128)(2,1)} %gather_fusion.3, pred[32]{0:T(512)(128)(4,1)S(1)} %compare_and_fusion.1, pred[32]{0:T(512)(128)(4,1)S(1)} %compare_bitcast_fusion), kind=kOutput, calls=%fused_computation.9 | convolution fusion | flops 271056896 | bytes 8388672 | tf_op jit(solution)/shard_map/kin,nkl->kil/dot_general | solution.py:48
  (25 shorter events, 0.5 us)
Async XLA Ops:
  7.2 113.3 %copy-start = (s32[1,64,32]{1,2,0:T(8,128)S(1)}, s32[1,64,32]{1,2,0:T(8,128)}, u32[]{:S(2)}) copy-start(s32[1,64,32]{1,2,0:T(8,128)} %param.13) | copy-start | bytes 24580
  51.0 63.4 %all-to-all-start = ((bf16[4,64,32,128]{3,2,0,1:T(8,128)(2,1)}), bf16[4,64,32,128]{3,2,0,1:T(8,128)(2,1)}, u32[]{:S(2)}, u32[]{:S(2)}) async-start(bf16[4,64,32,128]{3,2,0,1:T(8,128)(2,1)} %copy.35), calls=%async_computation | async-start | bytes 4194304 | tf_op jit(solution)/shard_map/all_to_all | solution.py:35
  65.2 54.7 %copy-start.5 = (s32[1,64]{1,0:T(1,128)S(1)}, s32[1,64]{1,0:T(1,128)}, u32[]{:S(2)}) copy-start(s32[1,64]{1,0:T(1,128)} %param.15) | copy-start | bytes 772
  114.4 56.7 %all-to-all-start.1 = ((bf16[4,64,32,128]{3,2,0,1:T(8,128)(2,1)}), bf16[4,64,32,128]{3,2,0,1:T(8,128)(2,1)S(1)}, u32[]{:S(2)}, u32[]{:S(2)}) async-start(bf16[4,64,32,128]{3,2,0,1:T(8,128)(2,1)} %copy.43), calls=%async_computation.1 | async-start | bytes 4194304 | tf_op jit(solution)/shard_map/all_to_all | solution.py:35
  119.8 53.7 %all-gather.5.cloned.1.call-start = ((), (), s32[]{:S(2)}) async-start(), calls=%async_computation.2 | async-start | bytes 1310720 | tf_op jit(solution)/shard_map/all_gather | solution.py:45
  121.3 4.2 %copy-start.3 = (f32[1,1,32,128,128]{4,3,2,1,0:T(8,128)S(1)}, f32[1,1,32,128,128]{4,3,2,1,0:T(8,128)}, u32[]{:S(2)}) copy-start(f32[1,1,32,128,128]{4,3,2,1,0:T(8,128)} %param.12) | copy-start | bytes 6291460
  124.2 1.3 copy-start.2
  133.6 4.7 %copy-start.4 = (bf16[2,256,256]{2,1,0:T(8,128)(2,1)S(1)}, bf16[2,256,256]{2,1,0:T(8,128)(2,1)}, u32[]{:S(2)}) copy-start(bf16[2,256,256]{2,1,0:T(8,128)(2,1)} %param.11) | copy-start | bytes 786436
  138.1 71.0 %all-gather.7.cloned.1.call-start = ((), (), s32[]{:S(2)}) async-start(), calls=%async_computation.3 | async-start | bytes 1310720 | tf_op jit(solution)/shard_map/all_gather | solution.py:45
  176.9 3.8 %copy-start.1 = (bf16[64,4,1,32,128]{4,1,0,3,2:T(4,128)(2,1)S(1)}, bf16[64,4,1,32,128]{4,1,0,3,2:T(4,128)(2,1)}, u32[]{:S(2)}) copy-start(bf16[64,4,1,32,128]{4,1,0,3,2:T(4,128)(2,1)} %copy.44) | copy-start | bytes 6291460
Sparse Core Ops, SparseCore 0:
  138.2 27.7 all-gather.4
  186.2 22.9 all-gather.6
